TPU v7x, 256 devices: a whole 4x4x8 slice. The times are simulated.
256 devices in a mesh: section: 8 (over z), expert: 32 (over x, y, core).
Axes of the slice: x: 4, y: 4, z: 8, core: 2. Of those that a mesh axis runs over, the one named last changes fastest.
Arguments:
- acts: bfloat16 [8, 8192, 2048], P('section', 'expert'), may hold values from -6 to 6
- expert_ids: int32 [8, 8192, 2], P('section', 'expert'), may hold values from 0 to 31, all different within a row; in each aligned block of 256 rows (0 to 255, 256 to 511, ..., all dimensions but the last counted through in order) at most 24 rows name the same one
- router: bfloat16 [8, 2048, 32], P('section'), may hold values from -0.125 to 0.125
- skip_gain: float32 [8, 2048], P('section'), may hold values from 0.5 to 1.5
- skip_rows: bfloat16 [8, 8192, 2048], P('section', 'expert'), may hold values from -6 to 6
- w_in: bfloat16 [8, 32, 2048, 1024], P('section', 'expert'), may hold values from -0.125 to 0.125
- w_out: bfloat16 [8, 32, 1024, 2048], P('section', 'expert'), may hold values from -0.1875 to 0.1875
Outputs:
- handed: bfloat16 [8, 8192, 2048], P('section', 'expert')
- mirrored: bfloat16 [8, 8192, 2048], P('section', 'expert')
Inputs may be any that keep to these rules, and one draw needn't show every extreme that they name: `expert_ids`: each token names 2 different experts. Among the 256 tokens of one group no expert is named more than 24 times, a bound that some block reaches.
All inputs are finite; a program needn't handle non-finite values.
Results may differ from a plain program's by a relative error of at most 0.0041.
Values may be sent and summed in bfloat16 or wider, within the bound.
A program may use at most 64 MiB of HBM per device.

v0:
```python
import jax
import jax.numpy as jnp
from jax import lax
from jax.sharding import PartitionSpec as P


def shifted(shard, axis, by):
    peers = lax.axis_size(axis)
    return lax.ppermute(shard, axis, [(i, (i + by) % peers) for i in range(peers)])


def rms(values):
    return values * lax.rsqrt(jnp.mean(values * values, axis=-1, keepdims=True) + 1e-06)


def slots_of(group_ids, experts):
    flat = group_ids.reshape(-1)
    onehot = (flat[:, None] == jnp.arange(experts, dtype=jnp.int32)[None, :]).astype(jnp.int32)
    before = jnp.cumsum(onehot, axis=0) - onehot
    return jnp.sum(before * onehot, axis=1)


def expert_apply(rows, first, second):
    width = rows.shape[-1]
    flat = rows.reshape(-1, width)
    hidden = jax.nn.gelu(
        jnp.dot(flat, first, preferred_element_type=jnp.float32), approximate=True
    ).astype(jnp.bfloat16)
    result = jnp.dot(hidden, second, preferred_element_type=jnp.float32).astype(jnp.bfloat16)
    return result.reshape(rows.shape)


def local(acts, expert_ids, router, skip_gain, skip_rows, w_in, w_out):
    section_pos = lax.axis_index("section")
    section_count = lax.axis_size("section")
    tokens = acts[0]
    group_ids = expert_ids[0]
    tok_count = tokens.shape[0]
    width = tokens.shape[1]
    topk = group_ids.shape[1]
    experts = router.shape[2]
    capacity = 3 * tok_count * topk // (2 * experts)
    decoder = section_pos >= section_count // 2
    skip_term = skip_gain[0][None, :] * rms(skip_rows[0].astype(jnp.float32))
    h_rows = tokens.astype(jnp.float32) + jnp.where(decoder, skip_term, jnp.zeros_like(skip_term))
    normed = rms(h_rows).astype(jnp.bfloat16)
    logits = jnp.dot(normed, router[0], preferred_element_type=jnp.float32)
    chosen = jnp.take_along_axis(logits, group_ids, axis=1)
    gates = jax.nn.softmax(chosen, axis=-1)
    slot = slots_of(group_ids, experts)
    target = group_ids.reshape(-1) * capacity + slot
    repeated = jnp.repeat(normed, topk, axis=0)
    buffer = jnp.zeros((experts * capacity, width), jnp.bfloat16).at[target].set(repeated)
    send_rows = buffer.reshape(experts, capacity, width)
    first = w_in[0, 0]
    second = w_out[0, 0]
    arrived = lax.all_to_all(send_rows, "expert", split_axis=0, concat_axis=0, tiled=True)
    worked = expert_apply(arrived, first, second)
    back_rows = lax.all_to_all(worked, "expert", split_axis=0, concat_axis=0, tiled=True)
    fetched = back_rows.reshape(experts * capacity, width)[target].reshape(tok_count, topk, width)
    combined = jnp.sum(gates[:, :, None] * fetched.astype(jnp.float32), axis=1)
    output_rows = (h_rows + combined).astype(jnp.bfloat16)
    handed = shifted(output_rows, "section", 1)
    pieces = output_rows.reshape(section_count, tok_count // section_count, width)
    spread = lax.all_to_all(pieces, "section", split_axis=0, concat_axis=0, tiled=True)
    collected = lax.all_to_all(spread[::-1], "section", split_axis=0, concat_axis=0, tiled=True)
    mirror_rows = collected.reshape(tok_count, width)
    return (handed[None], mirror_rows[None])


def solution(mesh):
    placed = (
        P("section", "expert", None),
        P("section", "expert", None),
        P("section", None, None),
        P("section", None),
        P("section", "expert", None),
        P("section", "expert", None, None),
        P("section", "expert", None, None),
    )
    return jax.shard_map(
        local,
        mesh=mesh,
        in_specs=placed,
        out_specs=(P("section", "expert", None), P("section", "expert", None)),
        check_vma=False,
    )
```

profile of v0, /device:TPU:33, one launch (start us, length us, event | category | flops | bytes accessed | tf_op | source)
XLA Modules:
  0.0 226.4 jit_solution(16680081298821900251)
XLA Ops:
  2.6 1.5 fusion.15
  4.2 1.9 multiply_reduce_fusion.1
  6.7 1.3 broadcast_in_dim.32
  8.0 2.2 reshape.243
  10.2 1.2 reduce-window.6
  12.1 5.7 %scatter_custom_fusion = bf16[768,2048]{1,0:T(8,128)(2,1)S(1)} fusion(s32[512]{0:T(512)S(1)} %bitcast.103, bf16[512,2048]{1,0:T(8,128)(2,1)} %reshape.243, bf16[]{:T(256)} %constant.30.clone.1), kind=kCustom, calls=%fused_computation.29 | custom fusion | bytes 3146240 | tf_op jit(solution)/shard_map/scatter | solution.py:53
  17.8 47.2 %all_to_all.20 = bf16[32,24,2048]{2,1,0:T(8,128)(2,1)S(1)} all-to-all(bf16[32,24,2048]{2,1,0:T(8,128)(2,1)S(1)} %bitcast.94), channel_id=1, replica_groups=mesh['section'=8,'expert'=32] {'expert'}, dimensions={0} | all-to-all | bytes 6291456 | tf_op jit(solution)/shard_map/all_to_all | solution.py:57
  65.0 4.0 %fusion.14 = bf16[768,1024]{1,0:T(8,128)(2,1)S(1)} fusion(bf16[768,2048]{1,0:T(8,128)(2,1)S(1)} %bitcast.96, bf16[1,1,2048,1024]{3,2,1,0:T(8,128)(2,1)S(1)} %copy-done.8), kind=kOutput, calls=%fused_computation.17 | convolution fusion | flops 3228303360 | bytes 8912896 | tf_op jit(solution)/shard_map/dot_general | solution.py:27
  69.0 4.8 %fusion.4 = bf16[768,2048]{1,0:T(8,128)(2,1)} fusion(bf16[768,1024]{1,0:T(8,128)(2,1)S(1)} %fusion.14, bf16[1,1,1024,2048]{3,2,1,0:T(8,128)(2,1)S(1)} %copy-done.9), kind=kOutput, calls=%fused_computation.9 | convolution fusion | flops 3222798336 | bytes 8912896 | tf_op jit(solution)/shard_map/dot_general | solution.py:29
  73.8 4.1 %all-to-all-start.1 = ((bf16[32,24,2048]{2,1,0:T(8,128)(2,1)}), bf16[32,24,2048]{2,1,0:T(8,128)(2,1)S(1)}, u32[]{:S(2)}, u32[]{:S(2)}) async-start(bf16[32,24,2048]{2,1,0:T(8,128)(2,1)} %bitcast.95), calls=%async_computation.1 | async-start | bytes 6291456 | tf_op jit(solution)/shard_map/all_to_all | solution.py:59
  79.8 2.3 fusion.24
  82.1 4.5 %gather_fusion.1 = f32[512]{0:T(512)S(1)} fusion(f32[256,32]{0,1:T(8,128)S(1)} %fusion.24, s32[512]{0:T(512)S(1)} %reshape.233), kind=kCustom, calls=%fused_computation.1 | custom fusion | bytes 8192 | tf_op jit(solution)/shard_map/jit(take_along_axis)/gather | solution.py:48
  89.5 1.7 fusion.27
  91.3 26.4 %all-to-all-done.1 = bf16[32,24,2048]{2,1,0:T(8,128)(2,1)S(1)} async-done(((bf16[32,24,2048]{2,1,0:T(8,128)(2,1)}), bf16[32,24,2048]{2,1,0:T(8,128)(2,1)S(1)}, u32[]{:S(2)}, u32[]{:S(2)}) %all-to-all-start.1) | async-done | bytes 3145760 | tf_op jit(solution)/shard_map/all_to_all | solution.py:59
  117.6 3.3 %gather_fusion = bf16[512,2048]{1,0:T(8,128)(2,1)} fusion(bf16[768,2048]{1,0:T(8,128)(2,1)S(1)} %bitcast.90, s32[1024]{0:T(1024)S(1)} %pad_clamp_fusion), kind=kCustom, calls=%fused_computation | custom fusion | bytes 4196352 | tf_op jit(solution)/shard_map/gather | solution.py:60
  120.9 5.5 %reshape.222 = f32[256,2,2048]{2,1,0:T(2,128)} reshape(bf16[512,2048]{1,0:T(8,128)(2,1)} %gather_fusion) | data formatting | bytes 6291456 | tf_op jit(solution)/shard_map/convert_element_type | solution.py:61
  126.4 8.9 %multiply_reduce_fusion = f32[256,2048]{1,0:T(8,128)S(1)} fusion(f32[256,2,2048]{2,1,0:T(2,128)} %reshape.222, f32[256,2]{1,0:T(8,128)S(1)} %copy-done.5), kind=kLoop, calls=%fused_computation.8 | loop fusion | flops 1572864 | bytes 6293504 | tf_op jit(solution)/shard_map/reduce_sum | solution.py:61
  136.0 33.5 %all_to_all.21 = bf16[8,32,2048]{2,1,0:T(8,128)(2,1)} all-to-all(bf16[8,32,2048]{2,1,0:T(8,128)(2,1)S(1)} %add_convert_fusion), channel_id=1, replica_groups=mesh['section'=8,'expert'=32] {'section'}, dimensions={0} | all-to-all | bytes 2097152 | tf_op jit(solution)/shard_map/all_to_all | solution.py:65
  169.5 2.3 %rev.3 = bf16[8,32,2048]{2,1,0:T(8,128)(2,1)} reverse(bf16[8,32,2048]{2,1,0:T(8,128)(2,1)} %all_to_all.21), dimensions={0} | reverse | bytes 2097152 | tf_op jit(solution)/shard_map/rev | solution.py:66
  171.8 5.9 %all-to-all-start.3 = ((bf16[8,32,2048]{2,1,0:T(8,128)(2,1)}), bf16[8,32,2048]{2,1,0:T(8,128)(2,1)}, u32[]{:S(2)}, u32[]{:S(2)}) async-start(bf16[8,32,2048]{2,1,0:T(8,128)(2,1)} %rev.3), calls=%async_computation.3 | async-start | bytes 2097152 | tf_op jit(solution)/shard_map/all_to_all | solution.py:66
  177.7 1.8 add_convert_fusion.1
  179.5 1.3 collective-permute-start
  180.8 42.3 %collective-permute-done = bf16[256,2048]{1,0:T(8,128)(2,1)S(1)} collective-permute-done((bf16[256,2048]{1,0:T(8,128)(2,1)S(1)}, bf16[256,2048]{1,0:T(8,128)(2,1)S(1)}, u32[]{:S(2)}, u32[]{:S(2)}) %collective-permute-start) | collective-permute-done | bytes 1048608 | tf_op jit(solution)/shard_map/ppermute | solution.py:9
  224.1 2.3 %copy.21 = bf16[1,256,2048]{2,1,0:T(8,128)(2,1)} copy(bf16[1,256,2048]{2,1,0:T(8,128)(2,1)} %bitcast.20) | data formatting | bytes 2097152
  (46 shorter events, 9.7 us)
Async XLA Ops:
  0.6 79.2 %copy-start = (bf16[1,2048,32]{1,2,0:T(8,128)(2,1)S(1)}, bf16[1,2048,32]{1,2,0:T(8,128)(2,1)}, u32[]{:S(2)}) copy-start(bf16[1,2048,32]{1,2,0:T(8,128)(2,1)} %param.9) | copy-start | bytes 393220
  0.6 3.5 %copy-start.1 = (bf16[1,256,2048]{2,1,0:T(8,128)(2,1)S(1)}, bf16[1,256,2048]{2,1,0:T(8,128)(2,1)}, u32[]{:S(2)}) copy-start(bf16[1,256,2048]{2,1,0:T(8,128)(2,1)} %param.11) | copy-start | bytes 3145732
  0.7 5.4 %copy-start.6 = (f32[1,2048]{1,0:T(1,128)S(1)}, f32[1,2048]{1,0:T(1,128)}, u32[]{:S(2)}) copy-start(f32[1,2048]{1,0:T(1,128)} %param.10) | copy-start | bytes 24580
  0.7 5.4 %copy-start.3 = (bf16[1,256,2048]{2,1,0:T(8,128)(2,1)S(1)}, bf16[1,256,2048]{2,1,0:T(8,128)(2,1)}, u32[]{:S(2)}) copy-start(bf16[1,256,2048]{2,1,0:T(8,128)(2,1)} %param.7) | copy-start | bytes 3145732
  17.8 47.2 %copy-start.8 = (bf16[1,1,2048,1024]{3,2,1,0:T(8,128)(2,1)S(1)}, bf16[1,1,2048,1024]{3,2,1,0:T(8,128)(2,1)}, u32[]{:S(2)}) copy-start(bf16[1,1,2048,1024]{3,2,1,0:T(8,128)(2,1)} %param.12) | copy-start | bytes 12582916
  65.0 4.0 %copy-start.9 = (bf16[1,1,1024,2048]{3,2,1,0:T(8,128)(2,1)S(1)}, bf16[1,1,1024,2048]{3,2,1,0:T(8,128)(2,1)}, u32[]{:S(2)}) copy-start(bf16[1,1,1024,2048]{3,2,1,0:T(8,128)(2,1)} %param.13) | copy-start | bytes 12582916
  73.8 4.1 %copy-start.7 = (s32[1,256,2]{1,2,0:T(2,128)S(1)}, s32[1,256,2]{1,2,0:T(2,128)}, u32[]{:S(2)}) copy-start(s32[1,256,2]{1,2,0:T(2,128)} %param.8) | copy-start | bytes 6148
  73.8 43.8 %all-to-all-start.1 = ((bf16[32,24,2048]{2,1,0:T(8,128)(2,1)}), bf16[32,24,2048]{2,1,0:T(8,128)(2,1)S(1)}, u32[]{:S(2)}, u32[]{:S(2)}) async-start(bf16[32,24,2048]{2,1,0:T(8,128)(2,1)} %bitcast.95), calls=%async_computation.1 | async-start | bytes 6291456 | tf_op jit(solution)/shard_map/all_to_all | solution.py:59
  120.9 5.5 %copy-start.5 = (f32[256,2]{1,0:T(8,128)S(1)}, f32[256,2]{1,0:T(8,128)}, u32[]{:S(2)}) copy-start(f32[256,2]{1,0:T(8,128)} %fusion.27) | copy-start | bytes 6148
  126.4 8.9 %copy-start.2 = (bf16[1,256,2048]{2,1,0:T(8,128)(2,1)S(1)}, bf16[1,256,2048]{2,1,0:T(8,128)(2,1)}, u32[]{:S(2)}) copy-start(bf16[1,256,2048]{2,1,0:T(8,128)(2,1)} %param.11) | copy-start | bytes 3145732
  126.4 8.9 %copy-start.4 = (bf16[1,256,2048]{2,1,0:T(8,128)(2,1)S(1)}, bf16[1,256,2048]{2,1,0:T(8,128)(2,1)}, u32[]{:S(2)}) copy-start(bf16[1,256,2048]{2,1,0:T(8,128)(2,1)} %param.7) | copy-start | bytes 3145732
  171.8 51.3 %all-to-all-start.3 = ((bf16[8,32,2048]{2,1,0:T(8,128)(2,1)}), bf16[8,32,2048]{2,1,0:T(8,128)(2,1)}, u32[]{:S(2)}, u32[]{:S(2)}) async-start(bf16[8,32,2048]{2,1,0:T(8,128)(2,1)} %rev.3), calls=%async_computation.3 | async-start | bytes 2097152 | tf_op jit(solution)/shard_map/all_to_all | solution.py:66
  179.5 43.5 %collective-permute-start = (bf16[256,2048]{1,0:T(8,128)(2,1)S(1)}, bf16[256,2048]{1,0:T(8,128)(2,1)S(1)}, u32[]{:S(2)}, u32[]{:S(2)}) collective-permute-start(bf16[256,2048]{1,0:T(8,128)(2,1)S(1)} %add_convert_fusion.1), channel_id=1, source_target_pairs={{0,32},{32,64},{64,96},{96,128},{128,160},{160,192},{192,224},{224... | collective-permute-start | bytes 3145736 | tf_op jit(solution)/shard_map/ppermute | solution.py:9
where the time goes:
time: 231 us; the launch traced here: 226 us
  blocking collectives  80.7 us (35%)
  waiting for transfers between devices  68.6 us (30%)
  local copies, waits for them, and re-layouts  32.6 us (14%)
  other arithmetic  21.3 us (9%)
  starting transfers between devices  11.3 us (5%)
  matrix products  11 us (5%)
    all_to_all x1, blocking collectives, local(): lax.all_to_all(send_rows, 'expert', split_axis=0, concat_axis=0, tiled=True)  47.2 us
    ppermute x1, waiting for transfers between devices, shifted(): lax.ppermute(shard, axis, [(i, (i + by) % peers) for i in range(peers)])  42.3 us
    all_to_all x1, blocking collectives, local(): lax.all_to_all(pieces, 'section', split_axis=0, concat_axis=0, tiled=True)  33.5 us
    all_to_all x1, waiting for transfers between devices, local(): lax.all_to_all(worked, 'expert', split_axis=0, concat_axis=0, tiled=True)  26.4 us
    reduce_sum x1, other arithmetic, local(): combined = jnp.sum(gates[:, :, None] * fetched.astype(jnp.float32), axis=1)  8.91 us
    gather x4, local copies, waits for them, and re-layouts, local(): chosen = jnp.take_along_axis(logits, group_ids, axis=1)  7.18 us
    all_to_all x1, starting transfers between devices, local(): lax.all_to_all(spread[::-1], 'section', split_axis=0, concat_axis=0, tile...  5.93 us
    scatter x1, local copies, waits for them, and re-layouts, local(): jnp.zeros((experts * capacity, width), jnp.bfloat16).at[target]  5.65 us
  transfers between devices with their start and end apart: 3, of which 2 were waited for; matrix products, arithmetic and copies ran while one was open for 7% of the time, Pallas kernels for 0%

commit v1 on v0

v1 whole, which is shorter than its diff:
```python
import functools

import jax
import jax.numpy as jnp
from jax import lax
from jax.experimental import pallas as pl
from jax.experimental.pallas import tpu as pltpu
from jax.sharding import PartitionSpec as P

MESH = pl.DeviceIdType.MESH
F32 = jnp.float32
BF16 = jnp.bfloat16

IN_CHUNKS = 2
OUT_CHUNKS = 8


def rms(values):
    return values * lax.rsqrt(jnp.mean(values * values, axis=-1, keepdims=True) + 1e-06)


def iota(shape, axis):
    return lax.broadcasted_iota(jnp.int32, shape, axis)


def partner(sides, me, i):
    nx, ny, nc = sides
    x, y, core = me // (ny * nc), (me // nc) % ny, me % nc
    a, c, b = i % nx, (i // nx) % nc, i // (nx * nc)
    return ((x + a) % nx) * (ny * nc) + ((y + a + b) % ny) * nc + (core + c) % nc


def kernel(
    sides, sections, experts, cap,
    acts, ids, router, gain, skip, w_in, w_out,
    handed, mirrored,
    wi, wo, h, normed, place, mix, send, recv, rows, acc, hidden, outs, back, ys,
    w_sem, own_sem, in_send, in_recv, out_send, out_recv, z_send, z_recv, dup_sem,
):
    sec = lax.axis_index("section")
    me = lax.axis_index("expert")
    tok, width = acts.shape
    ff = w_in.shape[1]
    slots = experts * cap
    nxt, mir = (sec + 1) % sections, sections - 1 - sec
    prv = (sec + sections - 1) % sections

    copy_wi = pltpu.make_async_copy(w_in, wi, w_sem.at[0])
    copy_wo = pltpu.make_async_copy(w_out, wo, w_sem.at[1])
    copy_wi.start()
    copy_wo.start()

    barrier = pltpu.get_barrier_semaphore()

    def greet(i, carry):
        pl.semaphore_signal(barrier, inc=1, device_id=(sec, partner(sides, me, i)), device_id_type=MESH)
        return carry

    lax.fori_loop(1, experts, greet, 0)
    pl.semaphore_signal(barrier, inc=1, device_id=(prv, me), device_id_type=MESH)
    pl.semaphore_signal(barrier, inc=1, device_id=(mir, me), device_id_type=MESH)

    decoder = (sec >= sections // 2).astype(F32)
    block = 32

    def norm_rows(i, carry):
        at = pl.ds(pl.multiple_of(i * block, block), block)
        term = gain[...] * rms(skip[at, :].astype(F32))
        value = acts[at, :].astype(F32) + jnp.where(decoder > 0.5, term, jnp.zeros_like(term))
        h[at, :] = value
        normed[at, :] = rms(value).astype(BF16)
        return carry

    lax.fori_loop(0, tok // block, norm_rows, 0)

    id0, id1 = ids[0:1, :], ids[1:2, :]
    kinds = iota((experts, tok), 0)
    one0, one1 = (id0 == kinds).astype(F32), (id1 == kinds).astype(F32)
    earlier = (iota((tok, tok), 0) < iota((tok, tok), 1)).astype(F32).astype(BF16)
    before = jnp.dot((one0 + one1).astype(BF16), earlier, preferred_element_type=F32)
    slot0 = jnp.sum(before * one0, axis=0, keepdims=True)
    slot1 = jnp.sum(before * one1, axis=0, keepdims=True)
    row0 = id0 * cap + slot0.astype(jnp.int32)
    row1 = id1 * cap + slot1.astype(jnp.int32)
    spots = iota((slots, tok), 0)
    place[...] = jnp.logical_or(spots == row0, spots == row1).astype(F32).astype(BF16)

    in_width = width // IN_CHUNKS
    peers = 8

    def own_copy(c):
        return pltpu.make_async_copy(send.at[c, me], recv.at[c, me], in_recv.at[c])

    for c in range(IN_CHUNKS):
        def fill(i, carry, c=c):
            at = pl.ds(pl.multiple_of(i * peers * cap, peers * cap), peers * cap)
            got = jnp.dot(place[at, :], normed[:, c * in_width:(c + 1) * in_width], preferred_element_type=F32)
            send[c, pl.ds(i * peers, peers)] = got.reshape(peers, cap, in_width).astype(BF16)
            return carry

        lax.fori_loop(0, experts // peers, fill, 0)
        if c == 0:
            pl.semaphore_wait(barrier, experts + 1)

        def dispatch(i, carry, c=c):
            to = partner(sides, me, i)
            pltpu.make_async_remote_copy(
                src_ref=send.at[c, to], dst_ref=recv.at[c, me],
                send_sem=in_send.at[c], recv_sem=in_recv.at[c],
                device_id=(sec, to), device_id_type=MESH,
            ).start()
            return carry

        lax.fori_loop(1, experts, dispatch, 0)
        own_copy(c).start()

    logits = jnp.dot(normed[...], router[...], preferred_element_type=F32)
    lines = iota((8, tok), 0)
    info = jnp.where(lines == 0, id0.astype(F32), jnp.where(lines == 1, id1.astype(F32), jnp.where(lines == 2, slot0, slot1)))
    eye = (iota((tok, tok), 0) == iota((tok, tok), 1)).astype(F32).astype(BF16)
    column = lax.dot_general(eye, info.astype(BF16), (((1,), (1,)), ((), ())), preferred_element_type=F32)
    names = iota((tok, experts), 1).astype(F32)
    chosen0 = jnp.sum(jnp.where(names == column[:, 0:1], logits, 0.0), axis=1, keepdims=True)
    chosen1 = jnp.sum(jnp.where(names == column[:, 1:2], logits, 0.0), axis=1, keepdims=True)
    top = jnp.maximum(chosen0, chosen1)
    exp0, exp1 = jnp.exp(chosen0 - top), jnp.exp(chosen1 - top)
    gate0, gate1 = exp0 / (exp0 + exp1), exp1 / (exp0 + exp1)
    spot0 = column[:, 0:1] * cap + column[:, 2:3]
    spot1 = column[:, 1:2] * cap + column[:, 3:4]
    along = iota((tok, slots), 1).astype(F32)
    gates = jnp.where(along == spot0, gate0, 0.0) + jnp.where(along == spot1, gate1, 0.0)
    high = gates.astype(BF16)
    mix[0:tok, :] = high
    mix[tok:, :] = (gates - high.astype(F32)).astype(BF16)

    copy_wi.wait()
    pair = 2
    tile = 256
    for c in range(IN_CHUNKS):
        pltpu.make_async_copy(send.at[c], recv.at[c], in_recv.at[c]).wait()
        span = pl.ds(c * in_width, in_width)

        def flatten(i, carry, c=c, span=span):
            at = pl.ds(pl.multiple_of(i * pair * cap, pair * cap), pair * cap)
            got = recv[c, pl.ds(i * pair, pair)].astype(F32)
            rows[at, span] = got.reshape(pair * cap, in_width).astype(BF16)
            return carry

        lax.fori_loop(0, experts // pair, flatten, 0)

        def first(n, carry, c=c, span=span):
            at = pl.ds(pl.multiple_of(n * tile, tile), tile)
            got = jnp.dot(rows[:, span], wi[span, at], preferred_element_type=F32)
            if c > 0:
                got = acc[:, at] + got
            if c < IN_CHUNKS - 1:
                acc[:, at] = got
            else:
                hidden[:, at] = jax.nn.gelu(got, approximate=True).astype(BF16)
            return carry

        lax.fori_loop(0, ff // tile, first, 0)

    copy_wo.wait()
    out_width = width // OUT_CHUNKS

    def second(c, carry):
        at = pl.ds(pl.multiple_of(c * out_width, out_width), out_width)
        got = jnp.dot(hidden[...], wo[:, at], preferred_element_type=F32)
        outs[c] = got.reshape(experts, cap, out_width).astype(BF16)

        def give_back(i, inner):
            to = partner(sides, me, i)
            pltpu.make_async_remote_copy(
                src_ref=outs.at[c, to], dst_ref=back.at[c, me],
                send_sem=out_send.at[c], recv_sem=out_recv.at[c],
                device_id=(sec, to), device_id_type=MESH,
            ).start()
            return inner

        lax.fori_loop(1, experts, give_back, 0)
        pltpu.make_async_copy(outs.at[c, me], back.at[c, me], out_recv.at[c]).start()
        return carry

    lax.fori_loop(0, OUT_CHUNKS, second, 0)

    def to_next(c):
        at = pl.ds(pl.multiple_of(c * out_width, out_width), out_width)
        return pltpu.make_async_remote_copy(
            src_ref=ys.at[c], dst_ref=handed.at[:, at],
            send_sem=z_send.at[0, c], recv_sem=z_recv.at[0, c],
            device_id=(nxt, me), device_id_type=MESH,
        )

    def to_mirror(c):
        at = pl.ds(pl.multiple_of(c * out_width, out_width), out_width)
        return pltpu.make_async_remote_copy(
            src_ref=ys.at[c], dst_ref=mirrored.at[:, at],
            send_sem=z_send.at[1, c], recv_sem=z_recv.at[1, c],
            device_id=(mir, me), device_id_type=MESH,
        )

    def double(c):
        at = pl.ds(pl.multiple_of(c * out_width, out_width), out_width)
        return pltpu.make_async_copy(handed.at[:, at], mirrored.at[:, at], dup_sem.at[c])

    sends_one = nxt == mir
    gets_one = prv == mir

    def combine(c, carry):
        pltpu.make_async_copy(outs.at[c], back.at[c], out_recv.at[c]).wait()
        at = pl.ds(pl.multiple_of(c * out_width, out_width), out_width)
        got = back[c].astype(F32).reshape(slots, out_width).astype(BF16)
        both = jnp.dot(mix[...], got, preferred_element_type=F32)
        ys[c] = (h[:, at] + (both[0:tok] + both[tok:])).astype(BF16)
        to_next(c).start()

        @pl.when(jnp.logical_not(sends_one))
        def _():
            to_mirror(c).start()

        return carry

    lax.fori_loop(0, OUT_CHUNKS, combine, 0)

    def arrive(c, carry):
        to_next(c).wait_recv()

        @pl.when(gets_one)
        def _():
            double(c).start()

        @pl.when(jnp.logical_not(gets_one))
        def _():
            to_mirror(c).wait_recv()

        return carry

    lax.fori_loop(0, OUT_CHUNKS, arrive, 0)

    def finish(c, carry):
        @pl.when(gets_one)
        def _():
            double(c).wait()

        to_next(c).wait_send()

        @pl.when(jnp.logical_not(sends_one))
        def _():
            to_mirror(c).wait_send()

        others = pl.ds(0, experts - 1)
        pltpu.make_async_copy(outs.at[c, others], back.at[c, others], out_send.at[c]).wait()
        return carry

    lax.fori_loop(0, OUT_CHUNKS, finish, 0)
    for c in range(IN_CHUNKS):
        others = pl.ds(0, experts - 1)
        pltpu.make_async_copy(send.at[c, others], recv.at[c, others], in_send.at[c]).wait()


def local(sides, acts, expert_ids, router, skip_gain, skip_rows, w_in, w_out):
    sections = lax.axis_size("section")
    tok, width = acts.shape[1], acts.shape[2]
    experts = router.shape[2]
    topk = expert_ids.shape[2]
    cap = 3 * tok * topk // (2 * experts)
    ff = w_in.shape[3]
    slots = experts * cap
    in_width, out_width = width // IN_CHUNKS, width // OUT_CHUNKS
    vmem = pl.BlockSpec(memory_space=pltpu.VMEM)
    hbm = pl.BlockSpec(memory_space=pl.ANY)
    out = jax.ShapeDtypeStruct((tok, width), BF16)
    dma = pltpu.SemaphoreType.DMA
    handed, mirrored = pl.pallas_call(
        functools.partial(kernel, sides, sections, experts, cap),
        out_shape=(out, out),
        in_specs=[vmem, vmem, vmem, vmem, vmem, hbm, hbm],
        out_specs=(vmem, vmem),
        scratch_shapes=[
            pltpu.VMEM((width, ff), BF16),
            pltpu.VMEM((ff, width), BF16),
            pltpu.VMEM((tok, width), F32),
            pltpu.VMEM((tok, width), BF16),
            pltpu.VMEM((slots, tok), BF16),
            pltpu.VMEM((2 * tok, slots), BF16),
            pltpu.VMEM((IN_CHUNKS, experts, cap, in_width), BF16),
            pltpu.VMEM((IN_CHUNKS, experts, cap, in_width), BF16),
            pltpu.VMEM((slots, width), BF16),
            pltpu.VMEM((slots, ff), F32),
            pltpu.VMEM((slots, ff), BF16),
            pltpu.VMEM((OUT_CHUNKS, experts, cap, out_width), BF16),
            pltpu.VMEM((OUT_CHUNKS, experts, cap, out_width), BF16),
            pltpu.VMEM((OUT_CHUNKS, tok, out_width), BF16),
            dma((2,)),
            dma,
            dma((IN_CHUNKS,)),
            dma((IN_CHUNKS,)),
            dma((OUT_CHUNKS,)),
            dma((OUT_CHUNKS,)),
            dma((2, OUT_CHUNKS)),
            dma((2, OUT_CHUNKS)),
            dma((OUT_CHUNKS,)),
        ],
        compiler_params=pltpu.CompilerParams(
            collective_id=0, has_side_effects=True, vmem_limit_bytes=60 * 1024 * 1024
        ),
        name="moe_window",
    )(acts[0], expert_ids[0].T, router[0], skip_gain, skip_rows[0], w_in[0, 0], w_out[0, 0])
    return (handed[None], mirrored[None])


def solution(mesh):
    placed = (
        P("section", "expert", None),
        P("section", "expert", None),
        P("section", None, None),
        P("section", None),
        P("section", "expert", None),
        P("section", "expert", None, None),
        P("section", "expert", None, None),
    )
    return jax.shard_map(
        functools.partial(local, (4, 4, 2)),
        mesh=mesh,
        in_specs=placed,
        out_specs=(P("section", "expert", None), P("section", "expert", None)),
        check_vma=False,
    )
```

time: 231 us -> 123 us (0.53); the launches traced: 226 us -> 123 us
  Pallas kernels: 0 us -> 115 us
  blocking collectives: 80.7 us -> 0 us
  waiting for transfers between devices: 68.6 us -> 0 us
  local copies, waits for them, and re-layouts: 32.6 us -> 6.52 us
  other arithmetic: 21.3 us -> 0 us
  starting transfers between devices: 11.3 us -> 0 us
  matrix products: 11 us -> 0 us
    pallas_call x0 -> x1, Pallas kernels: none -> 115 us  [local(): pl.pallas_call(functools.partial(kernel, sides, sections, experts, cap),...]
    all_to_all x2 -> x0, blocking collectives: 80.7 us -> none  [the longest x1 47.2 us: local(): lax.all_to_all(send_rows, 'expert', split_axis=0, concat_axis=0, tiled=True)]
    ppermute x1 -> x0, waiting for transfers between devices: 42.3 us -> none  [shifted(): lax.ppermute(shard, axis, [(i, (i + by) % peers) for i in range(peers)])]
    all_to_all x2 -> x0, waiting for transfers between devices: 26.4 us -> none  [the longest x1 26.4 us: local(): lax.all_to_all(worked, 'expert', split_axis=0, concat_axis=0, tiled=True)]
    reduce_sum x5 -> x0, other arithmetic: 13.5 us -> none  [the longest x1 8.91 us: local(): combined = jnp.sum(gates[:, :, None] * fetched.astype(jnp.float32), axis=1)]
    dot_general x3 -> x0, matrix products: 11 us -> none  [the longest x1 4.83 us: expert_apply(): jnp.dot(hidden, second, preferred_element_type=jnp.float32)]
    gather x5 -> x0, local copies, waits for them, and re-layouts: 10.5 us -> none  [the longest x4 7.18 us: local(): chosen = jnp.take_along_axis(logits, group_ids, axis=1)]
    all_to_all x2 -> x0, starting transfers between devices: 9.99 us -> none  [the longest x1 5.93 us: local(): lax.all_to_all(spread[::-1], 'section', split_axis=0, concat_axis=0, tile...]
  transfers between devices with their start and end apart: 3 -> 0, of which waited for: 2 -> 0; matrix products, arithmetic and copies ran while one was open for 7% -> 0% of each run, Pallas kernels for 0% -> 0%
where the time goes in v1:
time: 123 us
  Pallas kernels  115 us (93%)
  local copies, waits for them, and re-layouts  6.52 us (5%)
    pallas_call x1, Pallas kernels, local(): pl.pallas_call(functools.partial(kernel, sides, sections, experts, cap),...  115 us
    unnamed x3, local copies, waits for them, and re-layouts  6.52 us

profile of v1, /device:TPU:33, one launch (start us, length us, event | category | flops | bytes accessed | tf_op | source)
XLA Modules:
  0.0 122.5 jit_solution(12905895116487671727)
XLA Ops:
  0.6 1.9 %copy.9 = bf16[1,2048,32]{2,1,0:T(8,128)(2,1)} copy(bf16[1,2048,32]{1,2,0:T(8,128)(2,1)} %param.9) | data formatting | bytes 262144 | tf_op args[2]
  2.5 115.4 %moe_window.1 = (bf16[256,2048]{1,0:T(8,128)(2,1)}, bf16[256,2048]{1,0:T(8,128)(2,1)}) custom-call(bf16[256,2048]{1,0:T(8,128)(2,1)} %bitcast.15, s32[2,256]{1,0:T(2,128)} %bitcast.17, bf16[2048,32]{1,0:T(8,128)(2,1)} %bitcast.12, f32[1,2048]{1,0:T(1,128)} %gain.1, bf16[256,2048]{1,0:T(8,128)(2,1)} %bitcast.16, bf16[2048,1024]{1,0:T(8,128)(2,1)} %bitcast.10, ...), custom_call_target="tpu_custom_call" | custom-call | tf_op jit(solution)/shard_map/moe_window/pallas_call | solution.py:275
  117.9 2.3 %copy.12 = bf16[1,256,2048]{2,1,0:T(8,128)(2,1)} copy(bf16[1,256,2048]{2,1,0:T(8,128)(2,1)} %bitcast.14) | data formatting | bytes 2097152
  120.2 2.3 %copy.13 = bf16[1,256,2048]{2,1,0:T(8,128)(2,1)} copy(bf16[1,256,2048]{2,1,0:T(8,128)(2,1)} %bitcast.13) | data formatting | bytes 2097152

commit v2 on v1

v2 whole, which is shorter than its diff:
```python
import functools

import jax
import jax.numpy as jnp
from jax import lax
from jax.experimental import pallas as pl
from jax.experimental.pallas import tpu as pltpu
from jax.sharding import PartitionSpec as P

MESH = pl.DeviceIdType.MESH
F32 = jnp.float32
BF16 = jnp.bfloat16

IN_CHUNKS = 4
OUT_CHUNKS = 8
EARLY = 7
AFTER = (1, 3, 6)


def rms(values):
    return values * lax.rsqrt(jnp.mean(values * values, axis=-1, keepdims=True) + 1e-06)


def iota(shape, axis):
    return lax.broadcasted_iota(jnp.int32, shape, axis)


def partner(sides, chip, i):
    nx, ny = sides
    x, y, a, b = chip // ny, chip % ny, i % nx, i // nx
    return ((x + a) % nx) * ny + (y + a + b) % ny


def kernel(
    sides, sections, experts, cap,
    acts_in, ids_in, router_in, gain_in, skip_in, w_in, w_out,
    handed, mirrored,
    acts, ids, router, gain, skip, wi, wo, h, normed, place, mix, send, recv, rows, acc, hidden, outs, back, ys,
    w_sem, in_send, in_recv, out_send, out_recv, z_send, z_recv, dup_sem,
):
    sec = lax.axis_index("section")
    me = lax.axis_index("expert")
    core, chip = me % 2, me // 2
    chips = experts // 2
    first_core, second_core = core == 0, core == 1
    tok, width = acts.shape
    ff = w_in.shape[1]
    slots = experts * cap
    nxt, mir = (sec + 1) % sections, sections - 1 - sec
    prv = (sec + sections - 1) % sections

    loads = [
        pltpu.make_async_copy(source, target, w_sem.at[n])
        for n, (source, target) in enumerate((
            (acts_in, acts), (skip_in, skip), (gain_in, gain), (ids_in, ids),
            (router_in, router), (w_in, wi), (w_out, wo),
        ))
    ]
    for load in loads:
        load.start()
    copy_wi, copy_wo = loads[5], loads[6]

    barrier = pltpu.get_barrier_semaphore()

    def greet(i, carry):
        to = partner(sides, chip, i) * 2
        pl.semaphore_signal(barrier, inc=1, device_id=(sec, to), device_id_type=MESH)
        pl.semaphore_signal(barrier, inc=1, device_id=(sec, to + 1), device_id_type=MESH)
        return carry

    lax.fori_loop(1, chips, greet, 0)
    pl.semaphore_signal(barrier, inc=1, device_id=(sec, chip * 2 + 1 - core), device_id_type=MESH)
    pl.semaphore_signal(barrier, inc=1, device_id=(prv, me), device_id_type=MESH)
    pl.semaphore_signal(barrier, inc=1, device_id=(mir, me), device_id_type=MESH)

    for load in loads[0:3]:
        load.wait()
    decoder = (sec >= sections // 2).astype(F32)
    block = 32

    def norm_rows(i, carry):
        at = pl.ds(pl.multiple_of(i * block, block), block)
        term = gain[...] * rms(skip[at, :].astype(F32))
        value = acts[at, :].astype(F32) + jnp.where(decoder > 0.5, term, jnp.zeros_like(term))
        h[at, :] = value
        normed[at, :] = rms(value).astype(BF16)
        return carry

    lax.fori_loop(0, tok // block, norm_rows, 0)

    loads[3].wait()
    id0, id1 = ids[0:1, :], ids[1:2, :]
    kinds = iota((experts, tok), 0)
    one0, one1 = (id0 == kinds).astype(F32), (id1 == kinds).astype(F32)
    earlier = (iota((tok, tok), 0) < iota((tok, tok), 1)).astype(F32).astype(BF16)
    before = jnp.dot((one0 + one1).astype(BF16), earlier, preferred_element_type=F32)
    slot0 = jnp.sum(before * one0, axis=0, keepdims=True)
    slot1 = jnp.sum(before * one1, axis=0, keepdims=True)
    row0 = id0 * cap + slot0.astype(jnp.int32)
    row1 = id1 * cap + slot1.astype(jnp.int32)
    spots = iota((slots, tok), 0)
    place[...] = jnp.logical_or(spots == row0, spots == row1).astype(F32).astype(BF16)

    in_width = width // IN_CHUNKS
    peers = 8

    def dispatch(c):
        def to_core(to):
            pltpu.make_async_remote_copy(
                src_ref=send.at[c, to], dst_ref=recv.at[core, c, chip],
                send_sem=in_send.at[c], recv_sem=in_recv.at[core, c],
                device_id=(sec, to), device_id_type=MESH,
            ).start()

        def to_chip(i, carry):
            to = partner(sides, chip, i) * 2
            to_core(to + 1 - core)
            to_core(to + core)
            return carry

        lax.fori_loop(1, chips, to_chip, 0)
        to_core(chip * 2 + 1 - core)
        pltpu.make_async_copy(send.at[c, me], recv.at[core, c, chip], in_recv.at[core, c]).start()

    for c in range(IN_CHUNKS):
        def fill(i, carry, c=c):
            at = pl.ds(pl.multiple_of(i * peers * cap, peers * cap), peers * cap)
            got = jnp.dot(place[at, :], normed[:, c * in_width:(c + 1) * in_width], preferred_element_type=F32)
            send[c, pl.ds(i * peers, peers)] = got.reshape(peers, cap, in_width).astype(BF16)
            return carry

        lax.fori_loop(0, experts // peers, fill, 0)
        if c == 0:
            pl.semaphore_wait(barrier, experts + 1)

        @pl.when(first_core)
        def _(c=c):
            dispatch(c)

    loads[4].wait()
    logits = lax.dot_general(normed[...], router[...], (((1,), (1,)), ((), ())), preferred_element_type=F32)
    lines = iota((8, tok), 0)
    info = jnp.where(lines == 0, id0.astype(F32), jnp.where(lines == 1, id1.astype(F32), jnp.where(lines == 2, slot0, slot1)))
    eye = (iota((tok, tok), 0) == iota((tok, tok), 1)).astype(F32).astype(BF16)
    column = lax.dot_general(eye, info.astype(BF16), (((1,), (1,)), ((), ())), preferred_element_type=F32)
    names = iota((tok, experts), 1).astype(F32)
    chosen0 = jnp.sum(jnp.where(names == column[:, 0:1], logits, 0.0), axis=1, keepdims=True)
    chosen1 = jnp.sum(jnp.where(names == column[:, 1:2], logits, 0.0), axis=1, keepdims=True)
    top = jnp.maximum(chosen0, chosen1)
    exp0, exp1 = jnp.exp(chosen0 - top), jnp.exp(chosen1 - top)
    gate0, gate1 = exp0 / (exp0 + exp1), exp1 / (exp0 + exp1)
    spot0 = column[:, 0:1] * cap + column[:, 2:3]
    spot1 = column[:, 1:2] * cap + column[:, 3:4]
    along = iota((tok, slots), 1).astype(F32)
    gates = jnp.where(along == spot0, gate0, 0.0) + jnp.where(along == spot1, gate1, 0.0)
    high = gates.astype(BF16)
    mix[0:tok, :] = high
    mix[tok:, :] = (gates - high.astype(F32)).astype(BF16)

    copy_wi.wait()
    pair = 2
    tile = 256

    def enter(group):
        for c in range(IN_CHUNKS):
            pltpu.make_async_copy(recv.at[group, c], recv.at[group, c], in_recv.at[group, c]).wait()
            if group == 0 and c == IN_CHUNKS - 1:
                @pl.when(second_core)
                def _():
                    dispatch(0)

            span = pl.ds(c * in_width, in_width)

            def flatten(i, carry, c=c, span=span):
                at = pl.ds(pl.multiple_of(i * pair * cap, pair * cap), pair * cap)
                got = recv[group, c, pl.ds(i * pair, pair)].astype(F32)
                rows[at, span] = got.reshape(pair * cap, in_width).astype(BF16)
                return carry

            lax.fori_loop(0, chips // pair, flatten, 0)

            def first(n, carry, c=c, span=span):
                at = pl.ds(pl.multiple_of(n * tile, tile), tile)
                got = jnp.dot(rows[:, span], wi[span, at], preferred_element_type=F32)
                if c > 0:
                    got = acc[:, at] + got
                if c < IN_CHUNKS - 1:
                    acc[:, at] = got
                else:
                    hidden[:, at] = jax.nn.gelu(got, approximate=True).astype(BF16)
                return carry

            lax.fori_loop(0, ff // tile, first, 0)

    out_width = width // OUT_CHUNKS

    def leave(group, c):
        at = pl.ds(pl.multiple_of(c * out_width, out_width), out_width)
        got = jnp.dot(hidden[...], wo[:, at], preferred_element_type=F32)
        outs[group, c] = got.reshape(chips, cap, out_width).astype(BF16)

        def give_back(to):
            pltpu.make_async_remote_copy(
                src_ref=outs.at[group, c, to], dst_ref=back.at[c, me],
                send_sem=out_send.at[group, c], recv_sem=out_recv.at[c],
                device_id=(sec, to * 2 + group), device_id_type=MESH,
            ).start()

        def to_chip(i, carry):
            give_back(partner(sides, chip, i))
            return carry

        lax.fori_loop(1, chips, to_chip, 0)

        @pl.when(core == group)
        def _():
            pltpu.make_async_copy(outs.at[group, c, chip], back.at[c, me], out_recv.at[c]).start()

        @pl.when(core != group)
        def _():
            give_back(chip)

    def to_next(c):
        at = pl.ds(pl.multiple_of(c * out_width, out_width), out_width)
        return pltpu.make_async_remote_copy(
            src_ref=ys.at[c], dst_ref=handed.at[:, at],
            send_sem=z_send.at[0, c], recv_sem=z_recv.at[0, c],
            device_id=(nxt, me), device_id_type=MESH,
        )

    def to_mirror(c):
        at = pl.ds(pl.multiple_of(c * out_width, out_width), out_width)
        return pltpu.make_async_remote_copy(
            src_ref=ys.at[c], dst_ref=mirrored.at[:, at],
            send_sem=z_send.at[1, c], recv_sem=z_recv.at[1, c],
            device_id=(mir, me), device_id_type=MESH,
        )

    def double(c):
        at = pl.ds(pl.multiple_of(c * out_width, out_width), out_width)
        return pltpu.make_async_copy(handed.at[:, at], mirrored.at[:, at], dup_sem.at[c])

    sends_one = nxt == mir
    gets_one = prv == mir

    def combine(c, carry):
        pltpu.make_async_copy(back.at[c], back.at[c], out_recv.at[c]).wait()
        at = pl.ds(pl.multiple_of(c * out_width, out_width), out_width)
        got = back[c].astype(F32).reshape(slots, out_width).astype(BF16)
        both = jnp.dot(mix[...], got, preferred_element_type=F32)
        ys[c] = (h[:, at] + (both[0:tok] + both[tok:])).astype(BF16)
        to_next(c).start()

        @pl.when(jnp.logical_not(sends_one))
        def _():
            to_mirror(c).start()

        return carry

    enter(0)
    copy_wo.wait()

    def leave_first(c, carry):
        leave(0, c)
        for part, after in enumerate(AFTER):
            @pl.when(jnp.logical_and(second_core, c == after))
            def _(part=part):
                dispatch(part + 1)

        return carry

    lax.fori_loop(0, OUT_CHUNKS, leave_first, 0)

    @pl.when(first_core)
    def _():
        lax.fori_loop(0, EARLY, combine, 0)

    enter(1)

    def leave_second(c, carry):
        leave(1, c)
        return carry

    lax.fori_loop(0, OUT_CHUNKS, leave_second, 0)
    lax.fori_loop(jnp.where(first_core, EARLY, 0), OUT_CHUNKS, combine, 0)

    def arrive(c, carry):
        to_next(c).wait_recv()

        @pl.when(gets_one)
        def _():
            double(c).start()

        @pl.when(jnp.logical_not(gets_one))
        def _():
            to_mirror(c).wait_recv()

        return carry

    lax.fori_loop(0, OUT_CHUNKS, arrive, 0)

    def sent(group, c, count):
        some = pl.ds(0, count)
        pltpu.make_async_copy(outs.at[group, c, some], outs.at[group, c, some], out_send.at[group, c]).wait()

    def finish(c, carry):
        @pl.when(gets_one)
        def _():
            double(c).wait()

        to_next(c).wait_send()

        @pl.when(jnp.logical_not(sends_one))
        def _():
            to_mirror(c).wait_send()

        @pl.when(first_core)
        def _():
            sent(0, c, chips - 1)
            sent(1, c, chips)

        @pl.when(second_core)
        def _():
            sent(0, c, chips)
            sent(1, c, chips - 1)

        return carry

    lax.fori_loop(0, OUT_CHUNKS, finish, 0)
    for c in range(IN_CHUNKS):
        others = pl.ds(0, experts - 1)
        pltpu.make_async_copy(send.at[c, others], send.at[c, others], in_send.at[c]).wait()


def local(sides, acts, expert_ids, router, skip_gain, skip_rows, w_in, w_out):
    sections = lax.axis_size("section")
    tok, width = acts.shape[1], acts.shape[2]
    experts = router.shape[2]
    topk = expert_ids.shape[2]
    cap = 3 * tok * topk // (2 * experts)
    ff = w_in.shape[3]
    slots = experts * cap
    in_width, out_width = width // IN_CHUNKS, width // OUT_CHUNKS
    vmem = pl.BlockSpec(memory_space=pltpu.VMEM)
    hbm = pl.BlockSpec(memory_space=pltpu.HBM)
    out = jax.ShapeDtypeStruct((tok, width), BF16)
    dma = pltpu.SemaphoreType.DMA
    handed, mirrored = pl.pallas_call(
        functools.partial(kernel, sides, sections, experts, cap),
        out_shape=(out, out),
        in_specs=[hbm] * 7,
        out_specs=(vmem, vmem),
        scratch_shapes=[
            pltpu.VMEM((tok, width), BF16),
            pltpu.VMEM((topk, tok), jnp.int32),
            pltpu.VMEM((experts, width), BF16),
            pltpu.VMEM((1, width), F32),
            pltpu.VMEM((tok, width), BF16),
            pltpu.VMEM((width, ff), BF16),
            pltpu.VMEM((ff, width), BF16),
            pltpu.VMEM((tok, width), F32),
            pltpu.VMEM((tok, width), BF16),
            pltpu.VMEM((slots, tok), BF16),
            pltpu.VMEM((2 * tok, slots), BF16),
            pltpu.VMEM((IN_CHUNKS, experts, cap, in_width), BF16),
            pltpu.VMEM((2, IN_CHUNKS, experts // 2, cap, in_width), BF16),
            pltpu.VMEM((slots // 2, width), BF16),
            pltpu.VMEM((slots // 2, ff), F32),
            pltpu.VMEM((slots // 2, ff), BF16),
            pltpu.VMEM((2, OUT_CHUNKS, experts // 2, cap, out_width), BF16),
            pltpu.VMEM((OUT_CHUNKS, experts, cap, out_width), BF16),
            pltpu.VMEM((OUT_CHUNKS, tok, out_width), BF16),
            dma((7,)),
            dma((IN_CHUNKS,)),
            dma((2, IN_CHUNKS)),
            dma((2, OUT_CHUNKS)),
            dma((OUT_CHUNKS,)),
            dma((2, OUT_CHUNKS)),
            dma((2, OUT_CHUNKS)),
            dma((OUT_CHUNKS,)),
        ],
        compiler_params=pltpu.CompilerParams(
            collective_id=0, has_side_effects=True, vmem_limit_bytes=44 * 1024 * 1024
        ),
        name="moe_window",
    )(*(
        pltpu.with_memory_space_constraint(value, pltpu.HBM)
        for value in (acts[0], expert_ids[0].T, router[0].T, skip_gain, skip_rows[0], w_in[0, 0], w_out[0, 0])
    ))
    return (handed[None], mirrored[None])


def solution(mesh):
    placed = (
        P("section", "expert", None),
        P("section", "expert", None),
        P("section", None, None),
        P("section", None),
        P("section", "expert", None),
        P("section", "expert", None, None),
        P("section", "expert", None, None),
    )
    return jax.shard_map(
        functools.partial(local, (4, 4)),
        mesh=mesh,
        in_specs=placed,
        out_specs=(P("section", "expert", None), P("section", "expert", None)),
        check_vma=False,
    )
```

time: 123 us -> 108 us (0.88)
  Pallas kernels: 115 us -> 105 us
  local copies, waits for them, and re-layouts: 6.52 us -> 1.94 us
    pallas_call x1, Pallas kernels: 115 us -> 105 us  [local(): pl.pallas_call(functools.partial(kernel, sides, sections, experts, cap),...]
    unnamed x3 -> x2, local copies, waits for them, and re-layouts: 6.52 us -> 1.94 us
where the time goes in v2:
time: 108 us
  Pallas kernels  105 us (97%)
  local copies, waits for them, and re-layouts  1.94 us (2%)
    pallas_call x1, Pallas kernels, local(): pl.pallas_call(functools.partial(kernel, sides, sections, experts, cap),...  105 us

profile of v2, /device:TPU:33, one launch (start us, length us, event | category | flops | bytes accessed | tf_op | source)
XLA Modules:
  0.0 107.7 jit_solution(7310958815240211117)
XLA Ops:
  0.6 105.1 %moe_window.1 = (bf16[256,2048]{1,0:T(8,128)(2,1)S(1)}, bf16[256,2048]{1,0:T(8,128)(2,1)S(1)}) custom-call(bf16[256,2048]{1,0:T(8,128)(2,1)} %bitcast.16, s32[2,256]{1,0:T(2,128)} %bitcast.19, bf16[32,2048]{1,0:T(8,128)(2,1)} %bitcast.18, f32[1,2048]{1,0:T(1,128)} %gain_in.1, bf16[256,2048]{1,0:T(8,128)(2,1)} %bitcast.17, bf16[2048,1024]{1,0:T(8,128)(2,1)} %bitcast.14, ...), custom_call_target="tpu_custom_call" | custom-call | tf_op jit(solution)/shard_map/moe_window/pallas_call | solution.py:348
  105.8 1.0 copy.11
  106.7 1.0 copy.12

commit v3 on v2

--- a/solution.py
+++ b/solution.py
@@ -13,8 +13,10 @@
 
 IN_CHUNKS = 4
 OUT_CHUNKS = 8
-EARLY = 7
-AFTER = (1, 3, 6)
+EARLY = 6
+AFTER = (1, 3, 5)
+LEAD = 2
+GAP = 2
 
 
 def rms(values):
@@ -25,10 +27,12 @@
     return lax.broadcasted_iota(jnp.int32, shape, axis)
 
 
-def partner(sides, chip, i):
+def partners(sides, chip):
     nx, ny = sides
-    x, y, a, b = chip // ny, chip % ny, i % nx, i // nx
-    return ((x + a) % nx) * ny + (y + a + b) % ny
+    x, y = chip // ny, chip % ny
+    columns = [(x + a) % nx * ny for a in range(nx)]
+    lines = [(y + b) % ny for b in range(ny)]
+    return [columns[a] + lines[(a + b) % ny] for b in range(ny) for a in range(nx)]
 
 
 def kernel(
@@ -56,37 +60,19 @@
             (router_in, router), (w_in, wi), (w_out, wo),
         ))
     ]
-    for load in loads:
-        load.start()
+    for n in (3, 0, 1, 2, 4):
+        loads[n].start()
     copy_wi, copy_wo = loads[5], loads[6]
 
     barrier = pltpu.get_barrier_semaphore()
 
-    def greet(i, carry):
-        to = partner(sides, chip, i) * 2
-        pl.semaphore_signal(barrier, inc=1, device_id=(sec, to), device_id_type=MESH)
-        pl.semaphore_signal(barrier, inc=1, device_id=(sec, to + 1), device_id_type=MESH)
-        return carry
-
-    lax.fori_loop(1, chips, greet, 0)
+    around = partners(sides, chip)
+    for place_of in around[1:]:
+        for side in (0, 1):
+            pl.semaphore_signal(barrier, inc=1, device_id=(sec, place_of * 2 + side), device_id_type=MESH)
     pl.semaphore_signal(barrier, inc=1, device_id=(sec, chip * 2 + 1 - core), device_id_type=MESH)
     pl.semaphore_signal(barrier, inc=1, device_id=(prv, me), device_id_type=MESH)
     pl.semaphore_signal(barrier, inc=1, device_id=(mir, me), device_id_type=MESH)
-
-    for load in loads[0:3]:
-        load.wait()
-    decoder = (sec >= sections // 2).astype(F32)
-    block = 32
-
-    def norm_rows(i, carry):
-        at = pl.ds(pl.multiple_of(i * block, block), block)
-        term = gain[...] * rms(skip[at, :].astype(F32))
-        value = acts[at, :].astype(F32) + jnp.where(decoder > 0.5, term, jnp.zeros_like(term))
-        h[at, :] = value
-        normed[at, :] = rms(value).astype(BF16)
-        return carry
-
-    lax.fori_loop(0, tok // block, norm_rows, 0)
 
     loads[3].wait()
     id0, id1 = ids[0:1, :], ids[1:2, :]
@@ -101,6 +87,23 @@
     spots = iota((slots, tok), 0)
     place[...] = jnp.logical_or(spots == row0, spots == row1).astype(F32).astype(BF16)
 
+    for load in loads[0:3]:
+        load.wait()
+    copy_wi.start()
+    copy_wo.start()
+    decoder = (sec >= sections // 2).astype(F32)
+    block = 32
+
+    def norm_rows(i, carry):
+        at = pl.ds(pl.multiple_of(i * block, block), block)
+        term = gain[...] * rms(skip[at, :].astype(F32))
+        value = acts[at, :].astype(F32) + jnp.where(decoder > 0.5, term, jnp.zeros_like(term))
+        h[at, :] = value
+        normed[at, :] = rms(value).astype(BF16)
+        return carry
+
+    lax.fori_loop(0, tok // block, norm_rows, 0)
+
     in_width = width // IN_CHUNKS
     peers = 8
 
@@ -112,13 +115,9 @@
                 device_id=(sec, to), device_id_type=MESH,
             ).start()
 
-        def to_chip(i, carry):
-            to = partner(sides, chip, i) * 2
-            to_core(to + 1 - core)
-            to_core(to + core)
-            return carry
-
-        lax.fori_loop(1, chips, to_chip, 0)
+        for place_of in around[1:]:
+            to_core(place_of * 2 + 1 - core)
+            to_core(place_of * 2 + core)
         to_core(chip * 2 + 1 - core)
         pltpu.make_async_copy(send.at[c, me], recv.at[core, c, chip], in_recv.at[core, c]).start()
 
@@ -206,11 +205,8 @@
                 device_id=(sec, to * 2 + group), device_id_type=MESH,
             ).start()
 
-        def to_chip(i, carry):
-            give_back(partner(sides, chip, i))
-            return carry
-
-        lax.fori_loop(1, chips, to_chip, 0)
+        for place_of in around[1:]:
+            give_back(place_of)
 
         @pl.when(core == group)
         def _():
@@ -260,29 +256,41 @@
     enter(0)
     copy_wo.wait()
 
-    def leave_first(c, carry):
-        leave(0, c)
+    def begin(j, carry):
+        @pl.when(j < OUT_CHUNKS)
+        def _():
+            leave(0, j)
+
         for part, after in enumerate(AFTER):
-            @pl.when(jnp.logical_and(second_core, c == after))
+            @pl.when(jnp.logical_and(second_core, j == after))
             def _(part=part):
                 dispatch(part + 1)
 
-        return carry
-
-    lax.fori_loop(0, OUT_CHUNKS, leave_first, 0)
-
-    @pl.when(first_core)
-    def _():
-        lax.fori_loop(0, EARLY, combine, 0)
-
+        c = j - GAP
+
+        @pl.when(jnp.logical_and(first_core, jnp.logical_and(c >= 0, c < EARLY)))
+        def _():
+            combine(c, 0)
+
+        return carry
+
+    lax.fori_loop(0, max(OUT_CHUNKS, EARLY + GAP), begin, 0)
     enter(1)
 
-    def leave_second(c, carry):
-        leave(1, c)
-        return carry
-
-    lax.fori_loop(0, OUT_CHUNKS, leave_second, 0)
-    lax.fori_loop(jnp.where(first_core, EARLY, 0), OUT_CHUNKS, combine, 0)
+    def last(j, carry):
+        @pl.when(j < OUT_CHUNKS)
+        def _():
+            leave(1, j)
+
+        c = j + jnp.where(first_core, EARLY, -LEAD)
+
+        @pl.when(jnp.logical_and(c >= 0, c < OUT_CHUNKS))
+        def _():
+            combine(c, 0)
+
+        return carry
+
+    lax.fori_loop(0, OUT_CHUNKS + LEAD, last, 0)
 
     def arrive(c, carry):
         to_next(c).wait_recv()

time: 108 us -> 103 us (0.954)
  Pallas kernels: 105 us -> 101 us
    pallas_call x1, Pallas kernels: 105 us -> 101 us  [local(): pl.pallas_call(functools.partial(kernel, sides, sections, experts, cap),...]
where the time goes in v3:
time: 103 us
  Pallas kernels  101 us (98%)
  local copies, waits for them, and re-layouts  1.94 us (2%)
    pallas_call x1, Pallas kernels, local(): pl.pallas_call(functools.partial(kernel, sides, sections, experts, cap),...  101 us

profile of v3, /device:TPU:33, one launch (start us, length us, event | category | flops | bytes accessed | tf_op | source)
XLA Modules:
  0.0 103.3 jit_solution(18107837982014640222)
XLA Ops:
  0.6 100.7 %moe_window.1 = (bf16[256,2048]{1,0:T(8,128)(2,1)S(1)}, bf16[256,2048]{1,0:T(8,128)(2,1)S(1)}) custom-call(bf16[256,2048]{1,0:T(8,128)(2,1)} %bitcast.16, s32[2,256]{1,0:T(2,128)} %bitcast.19, bf16[32,2048]{1,0:T(8,128)(2,1)} %bitcast.18, f32[1,2048]{1,0:T(1,128)} %gain_in.1, bf16[256,2048]{1,0:T(8,128)(2,1)} %bitcast.17, bf16[2048,1024]{1,0:T(8,128)(2,1)} %bitcast.14, ...), custom_call_target="tpu_custom_call" | custom-call | tf_op jit(solution)/shard_map/moe_window/pallas_call | solution.py:356
  101.4 1.0 copy.11
  102.4 1.0 copy.12

commit v4 on v3

--- a/solution.py
+++ b/solution.py
@@ -32,7 +32,9 @@
     x, y = chip // ny, chip % ny
     columns = [(x + a) % nx * ny for a in range(nx)]
     lines = [(y + b) % ny for b in range(ny)]
-    return [columns[a] + lines[(a + b) % ny] for b in range(ny) for a in range(nx)]
+    steps = [(a, (a + b) % ny) for b in range(ny) for a in range(nx)]
+    reach = lambda step: min(step[0], nx - step[0]) + min(step[1], ny - step[1])
+    return [columns[a] + lines[b] for a, b in steps[:1] + sorted(steps[1:], key=reach, reverse=True)]
 
 
 def kernel(
@@ -102,7 +104,7 @@
         normed[at, :] = rms(value).astype(BF16)
         return carry
 
-    lax.fori_loop(0, tok // block, norm_rows, 0)
+    lax.fori_loop(0, tok // block, norm_rows, 0, unroll=2)
 
     in_width = width // IN_CHUNKS
     peers = 8
@@ -338,6 +340,17 @@
     for c in range(IN_CHUNKS):
         others = pl.ds(0, experts - 1)
         pltpu.make_async_copy(send.at[c, others], send.at[c, others], in_send.at[c]).wait()
+
+
+def store(first, second, first_out, second_out, sem):
+    copies = [
+        pltpu.make_async_copy(first, first_out, sem.at[0]),
+        pltpu.make_async_copy(second, second_out, sem.at[1]),
+    ]
+    for copy in copies:
+        copy.start()
+    for copy in copies:
+        copy.wait()
 
 
 def local(sides, acts, expert_ids, router, skip_gain, skip_rows, w_in, w_out):
@@ -395,6 +408,15 @@
         pltpu.with_memory_space_constraint(value, pltpu.HBM)
         for value in (acts[0], expert_ids[0].T, router[0].T, skip_gain, skip_rows[0], w_in[0, 0], w_out[0, 0])
     ))
+    handed, mirrored = pl.pallas_call(
+        store,
+        out_shape=(out, out),
+        in_specs=[vmem, vmem],
+        out_specs=(hbm, hbm),
+        scratch_shapes=[dma((2,))],
+        compiler_params=pltpu.CompilerParams(vmem_limit_bytes=8 * 1024 * 1024),
+        name="store",
+    )(handed, mirrored)
     return (handed[None], mirrored[None])
 
 

time: 103 us -> 101 us (0.981)
  local copies, waits for them, and re-layouts: 1.94 us -> 0 us
    unnamed x2 -> x0, local copies, waits for them, and re-layouts: 1.94 us -> none
    pallas_call x1, Pallas kernels: 101 us -> 98.9 us  [local(): pl.pallas_call(functools.partial(kernel, sides, sections, experts, cap),...]
    pallas_call x0 -> x1, Pallas kernels: none -> 1.33 us  [local(): pl.pallas_call(store, out_shape=(out, out), in_specs=[vmem, vmem], out_sp...]
where the time goes in v4:
time: 101 us
  Pallas kernels  100 us (99%)
    pallas_call x1, Pallas kernels, local(): pl.pallas_call(functools.partial(kernel, sides, sections, experts, cap),...  98.9 us

profile of v4, /device:TPU:33, one launch (start us, length us, event | category | flops | bytes accessed | tf_op | source)
XLA Modules:
  0.0 100.9 jit_solution(8651328477808045272)
XLA Ops:
  0.6 98.9 %moe_window.1 = (bf16[256,2048]{1,0:T(8,128)(2,1)S(1)}, bf16[256,2048]{1,0:T(8,128)(2,1)S(1)}) custom-call(bf16[256,2048]{1,0:T(8,128)(2,1)} %bitcast.14, s32[2,256]{1,0:T(2,128)} %bitcast.17, bf16[32,2048]{1,0:T(8,128)(2,1)} %bitcast.16, f32[1,2048]{1,0:T(1,128)} %gain_in.1, bf16[256,2048]{1,0:T(8,128)(2,1)} %bitcast.15, bf16[2048,1024]{1,0:T(8,128)(2,1)} %bitcast.12, ...), custom_call_target="tpu_custom_call" | custom-call | tf_op jit(solution)/shard_map/moe_window/pallas_call | solution.py:369
  99.5 1.3 %store.1 = (bf16[256,2048]{1,0:T(8,128)(2,1)}, bf16[256,2048]{1,0:T(8,128)(2,1)}) custom-call(bf16[256,2048]{1,0:T(8,128)(2,1)S(1)} %get-tuple-element.6.first, bf16[256,2048]{1,0:T(8,128)(2,1)S(1)} %get-tuple-element.7.second), custom_call_target="tpu_custom_call" | custom-call | tf_op jit(solution)/shard_map/store/pallas_call | solution.py:411

commit v5 on v4

--- a/solution.py
+++ b/solution.py
@@ -13,8 +13,8 @@
 
 IN_CHUNKS = 4
 OUT_CHUNKS = 8
-EARLY = 6
-AFTER = (1, 3, 5)
+EARLY = 7
+AFTER = (1, 3, 6)
 LEAD = 2
 GAP = 2
 
@@ -104,7 +104,7 @@
         normed[at, :] = rms(value).astype(BF16)
         return carry
 
-    lax.fori_loop(0, tok // block, norm_rows, 0, unroll=2)
+    lax.fori_loop(0, tok // block, norm_rows, 0, unroll=4)
 
     in_width = width // IN_CHUNKS
     peers = 8

time: 101 us -> 101 us (level)
  no operation moved by 1% of the time
where the time goes in v5:
time: 101 us
  Pallas kernels  100 us (99%)
    pallas_call x1, Pallas kernels, local(): pl.pallas_call(functools.partial(kernel, sides, sections, experts, cap),...  98.7 us

profile of v5, /device:TPU:33, one launch (start us, length us, event | category | flops | bytes accessed | tf_op | source)
XLA Modules:
  0.0 100.6 jit_solution(10306452255163692937)
XLA Ops:
  0.6 98.7 %moe_window.1 = (bf16[256,2048]{1,0:T(8,128)(2,1)S(1)}, bf16[256,2048]{1,0:T(8,128)(2,1)S(1)}) custom-call(bf16[256,2048]{1,0:T(8,128)(2,1)} %bitcast.14, s32[2,256]{1,0:T(2,128)} %bitcast.17, bf16[32,2048]{1,0:T(8,128)(2,1)} %bitcast.16, f32[1,2048]{1,0:T(1,128)} %gain_in.1, bf16[256,2048]{1,0:T(8,128)(2,1)} %bitcast.15, bf16[2048,1024]{1,0:T(8,128)(2,1)} %bitcast.12, ...), custom_call_target="tpu_custom_call" | custom-call | tf_op jit(solution)/shard_map/moe_window/pallas_call | solution.py:369
  99.3 1.3 %store.1 = (bf16[256,2048]{1,0:T(8,128)(2,1)}, bf16[256,2048]{1,0:T(8,128)(2,1)}) custom-call(bf16[256,2048]{1,0:T(8,128)(2,1)S(1)} %get-tuple-element.6.first, bf16[256,2048]{1,0:T(8,128)(2,1)S(1)} %get-tuple-element.7.second), custom_call_target="tpu_custom_call" | custom-call | tf_op jit(solution)/shard_map/store/pallas_call | solution.py:411
